TPU v7x, 256 devices: a whole 4x4x8 slice. The times are simulated.
256 devices in a mesh: tmpl: 64 (over z_lo, y, x, core), sta: 4 (over z_hi).
Axes of the slice: x: 4, y: 4, z: 8 (z_hi: 4, z_lo: 2; z = z_hi * 2 + z_lo), core: 2. Of those that a mesh axis runs over, the one named last changes fastest.
Arguments:
- window: bfloat16 [300, 8192], P('sta', 'tmpl'), may hold values from -6 to 6
- library: bfloat16 [64, 300, 300], P(None, 'sta'), may hold values from -6 to 6
- library_index: int32 [64], P('tmpl'), may hold values from 0 to 63
- moveout: int32 [64, 300], P('tmpl', 'sta'), may hold values from 0 to 212, as said below
- group_of: int32 [300], P('sta'), may hold values from 0 to 15, never falling along the last dimension, each value on 1 to 32 neighbouring positions
Outputs:
- stacks: bfloat16 [64, 16, 7680], P('tmpl', None, 'sta')
Inputs may be any that keep to these rules, and one draw needn't show every extreme that they name: Every row of moveout has some channel at 0 and some channel at 212.
All inputs are finite; a program needn't handle non-finite values.
Results may differ from a plain program's by a relative error of at most 0.01.
Values may be sent and summed in bfloat16 or wider, within the bound.
No kernel may reach another device: no remote copies, remote signals or barrier semaphores. Data moves between devices by JAX's collectives and lax.ppermute only.
A program may use at most 128 MiB of HBM per device.

v0:
```python
import jax
import jax.numpy as jnp
from jax import lax
from jax.experimental import pallas as pl
from jax.experimental.pallas import tpu as pltpu
from jax.sharding import PartitionSpec as P


TMPL_LEN = 300
GROUPS = 16
CHANS = 75
SIZES = (2, 4, 4, 2)
HELD = 10
ROWS = 80
PITCH = 72
BUNCH = 25

eps = 1e-06


def normalized_templates(library, library_index):
    chosen = lax.dynamic_index_in_dim(library, library_index[0], 0, keepdims=False).astype(jnp.float32)
    centered = chosen - jnp.mean(chosen, axis=-1, keepdims=True)
    factor = lax.rsqrt(jnp.mean(centered * centered, axis=-1, keepdims=True) + eps)
    return (centered * factor).astype(jnp.bfloat16)


def pairs_of(move):
    z_n, y_n, x_n, c_n = SIZES

    def index(z, y, x, c):
        return ((z * y_n + y) * x_n + x) * c_n + c

    pairs = []
    for z in range(z_n):
        for y in range(y_n):
            for x in range(x_n):
                for c in range(c_n):
                    tz, ty, tx, tc = move(z, y, x, c)
                    pairs.append((index(z, y, x, c), index(tz % z_n, ty % y_n, tx % x_n, tc % c_n)))
    return pairs


def spread(block, moves):
    came = [block]
    for move in moves:
        came.append(lax.ppermute(block, "tmpl", pairs_of(move)))
    return came


def join(blocks):
    return jnp.concatenate([block[None] for block in blocks])


def gather_window(window, taps, meta):
    came = lax.ppermute(window, "tmpl", pairs_of(lambda z, y, x, c: (z + 1, y, x, c)))
    fill = ((0, ROWS - CHANS), (0, 0))
    part = join([jnp.pad(window, fill), jnp.pad(came, fill)])
    part = join(spread(part, [lambda z, y, x, c, d=d: (z, y, x + d, c) for d in (1, 2, 3)]))
    part, taps, meta = lax.optimization_barrier((part.reshape(8, ROWS, 128), taps, meta))
    toep = toeplitz(taps, meta)
    part = spread(part, [lambda z, y, x, c, d=d: (z, y + d, x, c) for d in (1, 2, 3)])
    other = []
    for piece in part:
        other.append(lax.ppermute(piece, "tmpl", pairs_of(lambda z, y, x, c: (z, y, x, c + 1))))
    return part + other, toep, meta


def toeplitz_kernel(taps_ref, meta_ref, out_ref):
    def several(step, carry):
        for k in range(BUNCH):
            c = step * BUNCH + k
            base = jnp.broadcast_to(taps_ref[pl.ds(c, 1), :], (8, 512))
            for pair in range(8):
                halves = [
                    pltpu.roll(base, 16 * pair + 8 * h, axis=1, stride=1, stride_axis=0) for h in (0, 1)
                ]
                both = jnp.concatenate(halves, axis=0).astype(jnp.bfloat16)
                for q in range(4):
                    b = -q % 4
                    out_ref[c, 128 * q + 16 * pair : 128 * q + 16 * pair + 16, :] = both[:, 128 * b : 128 * b + 128]
        return carry

    lax.fori_loop(0, CHANS // BUNCH, several, 0)


def toeplitz(taps, meta):
    row = lax.broadcasted_iota(jnp.int32, (TMPL_LEN, 512), 0)
    column = lax.broadcasted_iota(jnp.int32, (TMPL_LEN, 512), 1)
    turned = jnp.dot(taps, (((row + column) & 511) == 0).astype(jnp.bfloat16), preferred_element_type=jnp.float32)
    return pl.pallas_call(
        toeplitz_kernel,
        out_shape=jax.ShapeDtypeStruct((CHANS, 512, 128), jnp.bfloat16),
        in_specs=[pl.BlockSpec(memory_space=pltpu.VMEM), pl.BlockSpec(memory_space=pl.ANY)],
        out_specs=pl.BlockSpec(memory_space=pltpu.VMEM),
        compiler_params=pltpu.CompilerParams(vmem_limit_bytes=16 << 20),
        cost_estimate=pl.CostEstimate(flops=CHANS * 65536 * 8, bytes_accessed=CHANS * 131072, transcendentals=0),
    )(turned, meta)


def correlate_kernel(
    meta_ref, m0_ref, m1_ref, m2_ref, m3_ref, n0_ref, n1_ref, n2_ref, n3_ref, toep_ref,
    o0_ref, o1_ref, o2_ref, o3_ref, rows_ref, inverse_ref, square_ref, shift_ref, acc_ref, band_ref,
):
    z0, y0, x0, c0, s0 = (meta_ref[k] for k in range(5))
    acc_ref[...] = jnp.zeros_like(acc_ref)
    band_ref[...] = window_band()
    square_ref[64 * ROWS : 65 * ROWS, :] = jnp.zeros((ROWS, 128), jnp.bfloat16)
    for r in (64, 65, 66):
        rows_ref[pl.ds(r, CHANS, stride=PITCH), :] = jnp.zeros((CHANS, 128), jnp.float32)
    pieces = ((m0_ref, n0_ref), (m1_ref, n1_ref), (m2_ref, n2_ref), (m3_ref, n3_ref))
    for dy, both in enumerate(pieces):
        for dx in range(4):
            for dz in range(2):
                spot = ((((z0 - dz) & 1) * 4 + ((y0 - dy) & 3)) * 4 + ((x0 - dx) & 3)) * 2
                for piece, i in zip(both, (spot + c0, spot + 1 - c0)):
                    block = piece[2 * dx + dz].astype(jnp.float32)
                    rows_ref[pl.ds(i, CHANS, stride=PITCH), :] = block[:CHANS]
                    square_ref[pl.ds(pl.multiple_of(i * ROWS, 16), ROWS), :] = (block * block).astype(jnp.bfloat16)

    carried = jnp.zeros((2 * ROWS, 128), jnp.float32)
    for part in reversed(range(8)):
        squares = jnp.concatenate(
            [square_ref[(8 * part + q) * ROWS : (8 * part + q + 8) * ROWS, :] for q in range(2)], axis=1
        )
        sums = lax.dot_general(
            squares, band_ref[...], (((1,), (0,)), ((), ())), preferred_element_type=jnp.float32
        )
        later = sums[:, 128:]
        total = sums[:, :128] + jnp.concatenate([later[2 * ROWS :], carried], axis=0)
        carried = later[: 2 * ROWS]
        inverse = lax.rsqrt(total * (1.0 / TMPL_LEN) + eps) * (1.0 / TMPL_LEN)
        for k in range(8):
            inverse_ref[pl.ds(8 * part + k, CHANS, stride=PITCH), :] = inverse[k * ROWS : k * ROWS + CHANS]

    lane = lax.broadcasted_iota(jnp.int32, (64, 128), 1)
    line = lax.broadcasted_iota(jnp.int32, (64, 128), 0)

    def bunch(step, carry):
        for k in range(BUNCH):
            c = step * BUNCH + k
            base = pl.multiple_of(c * PITCH, 8)
            values = jnp.concatenate(
                [rows_ref[pl.ds(base + q, 64), :].astype(jnp.bfloat16) for q in range(4)], axis=1
            )
            corr = lax.dot_general(
                values, toep_ref[c], (((1,), (0,)), ((), ())), preferred_element_type=jnp.float32
            )
            shift_ref[k, :64, :] = corr * inverse_ref[pl.ds(base, 64), :]
            move = meta_ref[5 + c]
            skip, turn = move >> 7, move & 127
            back = (128 - turn) & 127
            low = pltpu.roll(shift_ref[k, pl.ds(skip, 64), :], back, axis=1)
            high = pltpu.roll(shift_ref[k, pl.ds(skip + 1, 64), :], back, axis=1)
            moved = jnp.where(lane < 128 - turn, low, high)
            moved = jnp.where(line < 60, moved, 1.0)
            start = pl.multiple_of((meta_ref[5 + CHANS + c] - 2 * s0) * 64, 64)
            acc_ref[pl.ds(start, 64), :] += moved
        return carry

    lax.fori_loop(0, CHANS // BUNCH, bunch, 0)
    last = lax.broadcasted_iota(jnp.int32, (8, 128), 0) == 7
    for d, out in enumerate((o0_ref, o1_ref, o2_ref, o3_ref)):
        origin = ((s0 + d) & 3) * 15
        for g in range(HELD):
            upper = acc_ref[pl.ds(64 * g + origin, 8), :]
            lower = acc_ref[pl.ds(64 * g + origin + 8, 8), :]
            lower = jnp.where(last, acc_ref[64 * g + 56 : 64 * g + 64, :], lower)
            out[16 * g : 16 * g + 16, :] = jnp.concatenate([upper, lower], axis=0).astype(jnp.bfloat16)


def combine_kernel(p0_ref, p1_ref, p2_ref, p3_ref, out_ref, sum_ref):
    s0 = lax.axis_index("sta")
    sum_ref[...] = jnp.zeros_like(sum_ref)
    for d, part in enumerate((p0_ref, p1_ref, p2_ref, p3_ref)):
        start = pl.multiple_of(((s0 - d) & 3) * 32, 32)
        sum_ref[pl.ds(start, HELD * 16), :] += part[...].astype(jnp.float32)
    scale = jnp.sqrt(TMPL_LEN / sum_ref[pl.ds(15, GROUPS, stride=16), :])
    for r in range(15):
        rows = sum_ref[pl.ds(r, GROUPS, stride=16), :]
        out_ref[:, 128 * r : 128 * r + 128] = (rows * scale).astype(jnp.bfloat16)


def combine(parts):
    vmem = pl.BlockSpec(memory_space=pltpu.VMEM)
    return pl.pallas_call(
        combine_kernel,
        out_shape=jax.ShapeDtypeStruct((GROUPS, 1920), jnp.bfloat16),
        in_specs=[vmem] * 4,
        out_specs=vmem,
        scratch_shapes=[pltpu.VMEM((256, 128), jnp.float32)],
        compiler_params=pltpu.CompilerParams(vmem_limit_bytes=4 << 20),
    )(*parts)


def correlate(meta, pieces, toep):
    smem = pl.BlockSpec(memory_space=pltpu.SMEM)
    vmem = pl.BlockSpec(memory_space=pltpu.VMEM)
    return pl.pallas_call(
        correlate_kernel,
        out_shape=[jax.ShapeDtypeStruct((HELD * 16, 128), jnp.bfloat16)] * 4,
        in_specs=[smem] + [vmem] * 9,
        out_specs=[vmem] * 4,
        scratch_shapes=[
            pltpu.VMEM((CHANS * PITCH, 128), jnp.float32),
            pltpu.VMEM((CHANS * PITCH, 128), jnp.float32),
            pltpu.VMEM((65 * ROWS, 128), jnp.bfloat16),
            pltpu.VMEM((BUNCH, PITCH, 128), jnp.float32),
            pltpu.VMEM((HELD * 64, 128), jnp.float32),
            pltpu.VMEM((256, 256), jnp.bfloat16),
        ],
        compiler_params=pltpu.CompilerParams(vmem_limit_bytes=32 << 20),
    )(meta, *pieces, toep)


def window_band():
    column = lax.broadcasted_iota(jnp.int32, (256, 256), 1)
    late = column >= 128
    row = lax.broadcasted_iota(jnp.int32, (256, 256), 0) + jnp.where(late, 256, 0)
    first = column - jnp.where(late, 128, 0)
    return jnp.where((row >= first) & (row < first + TMPL_LEN), 1.0, 0.0).astype(jnp.bfloat16)


def on_device(window, library, library_index, moveout, group_of):
    me = lax.axis_index("tmpl")
    taps = normalized_templates(library, library_index)
    place = jnp.stack([me >> 5, (me >> 3) & 3, (me >> 1) & 3, me & 1, lax.axis_index("sta")]).astype(jnp.int32)
    meta = jnp.concatenate([place, moveout[0], group_of])
    pieces, toep, meta = gather_window(window, taps, meta)
    parts = correlate(meta, pieces, toep)
    came = [parts[0]]
    for d in (1, 2, 3):
        came.append(lax.ppermute(parts[d], "sta", [(i, (i + d) % 4) for i in range(4)]))
    return combine(came)[None]


def solution(mesh):
    in_specs = (P("sta", "tmpl"), P(None, "sta", None), P("tmpl"), P("tmpl", "sta"), P("sta"))
    out_specs = P("tmpl", None, "sta")

    return jax.shard_map(on_device, mesh=mesh, in_specs=in_specs, out_specs=out_specs, check_vma=False)
```

profile of v0, /device:TPU:1, one launch (start us, length us, event | category | flops | bytes accessed | tf_op | source)
XLA Modules:
  0.0 47.6 jit_solution(3815270536375833229)
XLA Ops:
  0.0 2.5 %collective-permute-start = (bf16[75,128]{1,0:T(8,128)(2,1)}, bf16[75,128]{1,0:T(8,128)(2,1)S(1)}, u32[]{:S(2)}, u32[]{:S(2)}) collective-permute-start(bf16[75,128]{1,0:T(8,128)(2,1)} %param.5), channel_id=1, source_target_pairs={{0,128},{4,132},{8,136},{12,140},{16,144},{20,148},{24,152},{28,15... | collective-permute-start | bytes 57608 | tf_op jit(solution)/shard_map/ppermute | solution.py:56
  3.1 1.1 %constant_dynamic-slice_fusion = bf16[1,75,300]{2,0,1:T(2,128)(2,1)S(1)} fusion(bf16[64,75,300]{2,0,1:T(8,128)(2,1)} %param.6, s32[]{:T(128)S(6)} %select_n.4), kind=kLoop, calls=%fused_computation.18 | loop fusion | bytes 90004 | tf_op jit(solution)/shard_map/jit(dynamic_index_in_dim)/dynamic_slice | solution.py:22
  4.3 0.1 convert_reduce_fusion
  4.4 0.2 fusion.6
  4.6 0.7 %pad_bitcast_fusion.1 = bf16[1,80,128]{2,1,0:T(8,128)(2,1)S(1)} fusion(bf16[75,128]{1,0:T(8,128)(2,1)} %param.5), kind=kLoop, calls=%fused_computation.14 | loop fusion | bytes 39680 | tf_op jit(solution)/shard_map/broadcast_in_dim | solution.py:52
  5.3 0.0 collective-permute-done
  5.4 2.8 %collective-permute-start.2 = (bf16[2,80,128]{2,1,0:T(8,128)(2,1)S(1)}, bf16[2,80,128]{2,1,0:T(8,128)(2,1)S(1)}, u32[]{:S(2)}, u32[]{:S(2)}) collective-permute-start(bf16[2,80,128]{2,1,0:T(8,128)(2,1)S(1)} %get-tuple-element.20), channel_id=1, source_target_pairs={{0,16},{4,20},{8,24},{12,28},{16,0},{20,4},{24,8},{28,12},{32,48},... | collective-permute-start | bytes 122888 | tf_op jit(solution)/shard_map/ppermute | solution.py:47
  8.2 0.3 collective-permute-start.1
  8.5 2.4 %collective-permute-start.3 = (bf16[2,80,128]{2,1,0:T(8,128)(2,1)S(1)}, bf16[2,80,128]{2,1,0:T(8,128)(2,1)S(1)}, u32[]{:S(2)}, u32[]{:S(2)}) collective-permute-start(bf16[2,80,128]{2,1,0:T(8,128)(2,1)S(1)} %get-tuple-element.20), channel_id=1, source_target_pairs={{0,24},{4,28},{8,0},{12,4},{16,8},{20,12},{24,16},{28,20},{32,56},... | collective-permute-start | bytes 122888 | tf_op jit(solution)/shard_map/ppermute | solution.py:47
  10.9 0.1 fusion.7
  11.0 0.8 %concatenate.11.meta_ref = s32[155]{0:T(256)S(1)} concatenate(s32[1]{0:T(128)} %bitcast.9, s32[1]{0:T(128)} %bitcast.10, s32[1]{0:T(128)} %bitcast.11, s32[1]{0:T(128)} %bitcast.12, s32[1]{0:T(128)} %bitcast.13, s32[75]{0:T(128)} %bitcast.42, s32[75]{0:T(128)} %param.9), dimensions={0} | concatenate | bytes 1240 | tf_op jit(solution)/shard_map/concatenate | solution.py:228
  11.7 0.0 collective-permute-done.2
  11.7 0.8 %collective-permute-done.1 = bf16[2,80,128]{2,1,0:T(8,128)(2,1)S(1)} collective-permute-done((bf16[2,80,128]{2,1,0:T(8,128)(2,1)S(1)}, bf16[2,80,128]{2,1,0:T(8,128)(2,1)S(1)}, u32[]{:S(2)}, u32[]{:S(2)}) %collective-permute-start.1) | collective-permute-done | bytes 40992 | tf_op jit(solution)/shard_map/ppermute | solution.py:47
  12.6 0.0 collective-permute-done.3
  12.6 2.5 %collective-permute-start.6 = (bf16[8,80,128]{2,1,0:T(8,128)(2,1)S(1)}, bf16[8,80,128]{2,1,0:T(8,128)(2,1)S(1)}, u32[]{:S(2)}, u32[]{:S(2)}) collective-permute-start(bf16[8,80,128]{2,1,0:T(8,128)(2,1)S(1)} %bitcast.34), channel_id=1, source_target_pairs={{0,96},{4,100},{8,104},{12,108},{16,112},{20,116},{24,120},{28,124... | collective-permute-start | bytes 491528 | tf_op jit(solution)/shard_map/ppermute | solution.py:47
  15.1 0.3 collective-permute-start.5
  15.4 0.7 %collective-permute-start.4 = (bf16[8,80,128]{2,1,0:T(8,128)(2,1)S(1)}, bf16[8,80,128]{2,1,0:T(8,128)(2,1)S(1)}, u32[]{:S(2)}, u32[]{:S(2)}) collective-permute-start(bf16[8,80,128]{2,1,0:T(8,128)(2,1)S(1)} %bitcast.36), channel_id=1, source_target_pairs={{0,32},{4,36},{8,40},{12,44},{16,48},{20,52},{24,56},{28,60},{32,6... | collective-permute-start | bytes 491528 | tf_op jit(solution)/shard_map/ppermute | solution.py:47
  16.1 3.2 %collective-permute-start.7 = (bf16[8,80,128]{2,1,0:T(8,128)(2,1)S(1)}, bf16[8,80,128]{2,1,0:T(8,128)(2,1)S(1)}, u32[]{:S(2)}, u32[]{:S(2)}) collective-permute-start(bf16[8,80,128]{2,1,0:T(8,128)(2,1)S(1)} %bitcast.37), channel_id=1, source_target_pairs={{0,4},{4,0},{8,12},{12,8},{16,20},{20,16},{24,28},{28,24},{32,36},... | collective-permute-start | bytes 491528 | tf_op jit(solution)/shard_map/ppermute | solution.py:65
  19.4 0.0 collective-permute-done.6.m3_ref
  19.4 3.7 %collective-permute-start.10 = (bf16[8,80,128]{2,1,0:T(8,128)(2,1)S(1)}, bf16[8,80,128]{2,1,0:T(8,128)(2,1)S(1)}, u32[]{:S(2)}, u32[]{:S(2)}) collective-permute-start(bf16[8,80,128]{2,1,0:T(8,128)(2,1)S(1)} %collective-permute-done.6.m3_ref), channel_id=1, source_target_pairs={{0,4},{4,0},{8,12},{12,8},{16,20},{20,16},{24,28},{28,24},{32,36},... | collective-permute-start | bytes 491528 | tf_op jit(solution)/shard_map/ppermute | solution.py:65
  23.0 0.0 collective-permute-done.5.m2_ref
  23.1 2.0 %collective-permute-start.9 = (bf16[8,80,128]{2,1,0:T(8,128)(2,1)S(1)}, bf16[8,80,128]{2,1,0:T(8,128)(2,1)S(1)}, u32[]{:S(2)}, u32[]{:S(2)}) collective-permute-start(bf16[8,80,128]{2,1,0:T(8,128)(2,1)S(1)} %collective-permute-done.5.m2_ref), channel_id=1, source_target_pairs={{0,4},{4,0},{8,12},{12,8},{16,20},{20,16},{24,28},{28,24},{32,36},... | collective-permute-start | bytes 491528 | tf_op jit(solution)/shard_map/ppermute | solution.py:65
  25.1 0.0 collective-permute-done.4.m1_ref
  25.1 1.6 %collective-permute-start.8 = (bf16[8,80,128]{2,1,0:T(8,128)(2,1)S(1)}, bf16[8,80,128]{2,1,0:T(8,128)(2,1)S(1)}, u32[]{:S(2)}, u32[]{:S(2)}) collective-permute-start(bf16[8,80,128]{2,1,0:T(8,128)(2,1)S(1)} %collective-permute-done.4.m1_ref), channel_id=1, source_target_pairs={{0,4},{4,0},{8,12},{12,8},{16,20},{20,16},{24,28},{28,24},{32,36},... | collective-permute-start | bytes 491528 | tf_op jit(solution)/shard_map/ppermute | solution.py:65
  26.7 0.2 fusion.taps_ref
  26.9 2.7 %shard_map.55.toep_ref = bf16[75,512,128]{2,1,0:T(8,128)(2,1)S(1)} custom-call(f32[75,512]{1,0:T(8,128)S(1)} %fusion.taps_ref, s32[155]{0:T(256)S(1)} %concatenate.11.meta_ref), custom_call_target="tpu_custom_call" | custom-call | flops 39321600 | bytes 9830400 | tf_op jit(solution)/shard_map/pallas_call | solution.py:91
  29.7 0.0 collective-permute-done.7.n0_ref
  29.7 0.0 collective-permute-done.10.n3_ref
  29.7 0.0 collective-permute-done.9.n2_ref
  29.7 0.0 collective-permute-done.8.n1_ref
  29.7 5.4 %shard_map.56 = (bf16[160,128]{1,0:T(8,128)(2,1)S(1)}, bf16[160,128]{1,0:T(8,128)(2,1)S(1)}, bf16[160,128]{1,0:T(8,128)(2,1)S(1)}, bf16[160,128]{1,0:T(8,128)(2,1)S(1)}) custom-call(s32[155]{0:T(256)S(1)} %concatenate.11.meta_ref, bf16[8,80,128]{2,1,0:T(8,128)(2,1)S(1)} %bitcast.38, bf16[8,80,128]{2,1,0:T(8,128)(2,1)S(1)} %collective-permute-done.4.m1_ref, ...), custom_call_target="tpu_custom_call" | custom-call | tf_op jit(solution)/shard_map/pallas_call | solution.py:199
  35.1 3.1 %collective-permute-start.11 = (bf16[160,128]{1,0:T(8,128)(2,1)S(1)}, bf16[160,128]{1,0:T(8,128)(2,1)S(1)}, u32[]{:S(2)}, u32[]{:S(2)}) collective-permute-start(bf16[160,128]{1,0:T(8,128)(2,1)S(1)} %get-tuple-element.16), channel_id=1, source_target_pairs={{0,1},{1,2},{2,3},{3,0},{4,5},{5,6},{6,7},{7,4},{8,9},{9,10},{10,1... | collective-permute-start | bytes 122888 | tf_op jit(solution)/shard_map/ppermute | solution.py:233
  38.2 4.2 %collective-permute-start.12 = (bf16[160,128]{1,0:T(8,128)(2,1)S(1)}, bf16[160,128]{1,0:T(8,128)(2,1)S(1)}, u32[]{:S(2)}, u32[]{:S(2)}) collective-permute-start(bf16[160,128]{1,0:T(8,128)(2,1)S(1)} %get-tuple-element.17), channel_id=1, source_target_pairs={{0,2},{1,3},{2,0},{3,1},{4,6},{5,7},{6,4},{7,5},{8,10},{9,11},{10,... | collective-permute-start | bytes 122888 | tf_op jit(solution)/shard_map/ppermute | solution.py:233
  42.4 2.4 %collective-permute-start.13 = (bf16[160,128]{1,0:T(8,128)(2,1)S(1)}, bf16[160,128]{1,0:T(8,128)(2,1)S(1)}, u32[]{:S(2)}, u32[]{:S(2)}) collective-permute-start(bf16[160,128]{1,0:T(8,128)(2,1)S(1)} %get-tuple-element.18), channel_id=1, source_target_pairs={{0,3},{1,0},{2,1},{3,2},{4,7},{5,4},{6,5},{7,6},{8,11},{9,8},{10,9... | collective-permute-start | bytes 122888 | tf_op jit(solution)/shard_map/ppermute | solution.py:233
  44.8 0.0 collective-permute-done.11.p1_ref
  44.8 0.2 collective-permute-done.12.p2_ref
  45.0 1.9 %collective-permute-done.13.p3_ref = bf16[160,128]{1,0:T(8,128)(2,1)S(1)} collective-permute-done((bf16[160,128]{1,0:T(8,128)(2,1)S(1)}, bf16[160,128]{1,0:T(8,128)(2,1)S(1)}, u32[]{:S(2)}, u32[]{:S(2)}) %collective-permute-start.13) | collective-permute-done | bytes 40992 | tf_op jit(solution)/shard_map/ppermute | solution.py:233
  46.8 0.7 %shard_map.57 = bf16[16,1920]{1,0:T(8,128)(2,1)} custom-call(bf16[160,128]{1,0:T(8,128)(2,1)S(1)} %get-tuple-element.15.p0_ref, bf16[160,128]{1,0:T(8,128)(2,1)S(1)} %collective-permute-done.11.p1_ref, bf16[160,128]{1,0:T(8,128)(2,1)S(1)} %collective-permute-done.12.p2_ref, bf16[160,128]{1,0:T(8,128)(2,1)S(1)} %collective-permute-done.13.p3_ref), custom_call_target="tpu_custom_call" | custom-call | tf_op jit(solution)/shard_map/pallas_call | solution.py:186
  (5 shorter events, 0.0 us)
Async XLA Ops:
  0.0 5.3 %collective-permute-start = (bf16[75,128]{1,0:T(8,128)(2,1)}, bf16[75,128]{1,0:T(8,128)(2,1)S(1)}, u32[]{:S(2)}, u32[]{:S(2)}) collective-permute-start(bf16[75,128]{1,0:T(8,128)(2,1)} %param.5), channel_id=1, source_target_pairs={{0,128},{4,132},{8,136},{12,140},{16,144},{20,148},{24,152},{28,15... | collective-permute-start | bytes 57608 | tf_op jit(solution)/shard_map/ppermute | solution.py:56
  5.4 6.4 %collective-permute-start.2 = (bf16[2,80,128]{2,1,0:T(8,128)(2,1)S(1)}, bf16[2,80,128]{2,1,0:T(8,128)(2,1)S(1)}, u32[]{:S(2)}, u32[]{:S(2)}) collective-permute-start(bf16[2,80,128]{2,1,0:T(8,128)(2,1)S(1)} %get-tuple-element.20), channel_id=1, source_target_pairs={{0,16},{4,20},{8,24},{12,28},{16,0},{20,4},{24,8},{28,12},{32,48},... | collective-permute-start | bytes 122888 | tf_op jit(solution)/shard_map/ppermute | solution.py:47
  8.2 4.4 %collective-permute-start.1 = (bf16[2,80,128]{2,1,0:T(8,128)(2,1)S(1)}, bf16[2,80,128]{2,1,0:T(8,128)(2,1)S(1)}, u32[]{:S(2)}, u32[]{:S(2)}) collective-permute-start(bf16[2,80,128]{2,1,0:T(8,128)(2,1)S(1)} %get-tuple-element.20), channel_id=1, source_target_pairs={{0,8},{4,12},{8,16},{12,20},{16,24},{20,28},{24,0},{28,4},{32,40},... | collective-permute-start | bytes 122888 | tf_op jit(solution)/shard_map/ppermute | solution.py:47
  8.5 4.1 %collective-permute-start.3 = (bf16[2,80,128]{2,1,0:T(8,128)(2,1)S(1)}, bf16[2,80,128]{2,1,0:T(8,128)(2,1)S(1)}, u32[]{:S(2)}, u32[]{:S(2)}) collective-permute-start(bf16[2,80,128]{2,1,0:T(8,128)(2,1)S(1)} %get-tuple-element.20), channel_id=1, source_target_pairs={{0,24},{4,28},{8,0},{12,4},{16,8},{20,12},{24,16},{28,20},{32,56},... | collective-permute-start | bytes 122888 | tf_op jit(solution)/shard_map/ppermute | solution.py:47
  12.6 6.8 %collective-permute-start.6 = (bf16[8,80,128]{2,1,0:T(8,128)(2,1)S(1)}, bf16[8,80,128]{2,1,0:T(8,128)(2,1)S(1)}, u32[]{:S(2)}, u32[]{:S(2)}) collective-permute-start(bf16[8,80,128]{2,1,0:T(8,128)(2,1)S(1)} %bitcast.34), channel_id=1, source_target_pairs={{0,96},{4,100},{8,104},{12,108},{16,112},{20,116},{24,120},{28,124... | collective-permute-start | bytes 491528 | tf_op jit(solution)/shard_map/ppermute | solution.py:47
  15.1 8.0 %collective-permute-start.5 = (bf16[8,80,128]{2,1,0:T(8,128)(2,1)S(1)}, bf16[8,80,128]{2,1,0:T(8,128)(2,1)S(1)}, u32[]{:S(2)}, u32[]{:S(2)}) collective-permute-start(bf16[8,80,128]{2,1,0:T(8,128)(2,1)S(1)} %bitcast.35), channel_id=1, source_target_pairs={{0,64},{4,68},{8,72},{12,76},{16,80},{20,84},{24,88},{28,92},{32,9... | collective-permute-start | bytes 491528 | tf_op jit(solution)/shard_map/ppermute | solution.py:47
  15.4 9.6 %collective-permute-start.4 = (bf16[8,80,128]{2,1,0:T(8,128)(2,1)S(1)}, bf16[8,80,128]{2,1,0:T(8,128)(2,1)S(1)}, u32[]{:S(2)}, u32[]{:S(2)}) collective-permute-start(bf16[8,80,128]{2,1,0:T(8,128)(2,1)S(1)} %bitcast.36), channel_id=1, source_target_pairs={{0,32},{4,36},{8,40},{12,44},{16,48},{20,52},{24,56},{28,60},{32,6... | collective-permute-start | bytes 491528 | tf_op jit(solution)/shard_map/ppermute | solution.py:47
  16.1 13.5 %collective-permute-start.7 = (bf16[8,80,128]{2,1,0:T(8,128)(2,1)S(1)}, bf16[8,80,128]{2,1,0:T(8,128)(2,1)S(1)}, u32[]{:S(2)}, u32[]{:S(2)}) collective-permute-start(bf16[8,80,128]{2,1,0:T(8,128)(2,1)S(1)} %bitcast.37), channel_id=1, source_target_pairs={{0,4},{4,0},{8,12},{12,8},{16,20},{20,16},{24,28},{28,24},{32,36},... | collective-permute-start | bytes 491528 | tf_op jit(solution)/shard_map/ppermute | solution.py:65
  19.4 10.3 %collective-permute-start.10 = (bf16[8,80,128]{2,1,0:T(8,128)(2,1)S(1)}, bf16[8,80,128]{2,1,0:T(8,128)(2,1)S(1)}, u32[]{:S(2)}, u32[]{:S(2)}) collective-permute-start(bf16[8,80,128]{2,1,0:T(8,128)(2,1)S(1)} %collective-permute-done.6.m3_ref), channel_id=1, source_target_pairs={{0,4},{4,0},{8,12},{12,8},{16,20},{20,16},{24,28},{28,24},{32,36},... | collective-permute-start | bytes 491528 | tf_op jit(solution)/shard_map/ppermute | solution.py:65
  23.1 6.6 %collective-permute-start.9 = (bf16[8,80,128]{2,1,0:T(8,128)(2,1)S(1)}, bf16[8,80,128]{2,1,0:T(8,128)(2,1)S(1)}, u32[]{:S(2)}, u32[]{:S(2)}) collective-permute-start(bf16[8,80,128]{2,1,0:T(8,128)(2,1)S(1)} %collective-permute-done.5.m2_ref), channel_id=1, source_target_pairs={{0,4},{4,0},{8,12},{12,8},{16,20},{20,16},{24,28},{28,24},{32,36},... | collective-permute-start | bytes 491528 | tf_op jit(solution)/shard_map/ppermute | solution.py:65
  25.1 4.6 %collective-permute-start.8 = (bf16[8,80,128]{2,1,0:T(8,128)(2,1)S(1)}, bf16[8,80,128]{2,1,0:T(8,128)(2,1)S(1)}, u32[]{:S(2)}, u32[]{:S(2)}) collective-permute-start(bf16[8,80,128]{2,1,0:T(8,128)(2,1)S(1)} %collective-permute-done.4.m1_ref), channel_id=1, source_target_pairs={{0,4},{4,0},{8,12},{12,8},{16,20},{20,16},{24,28},{28,24},{32,36},... | collective-permute-start | bytes 491528 | tf_op jit(solution)/shard_map/ppermute | solution.py:65
  35.1 9.7 %collective-permute-start.11 = (bf16[160,128]{1,0:T(8,128)(2,1)S(1)}, bf16[160,128]{1,0:T(8,128)(2,1)S(1)}, u32[]{:S(2)}, u32[]{:S(2)}) collective-permute-start(bf16[160,128]{1,0:T(8,128)(2,1)S(1)} %get-tuple-element.16), channel_id=1, source_target_pairs={{0,1},{1,2},{2,3},{3,0},{4,5},{5,6},{6,7},{7,4},{8,9},{9,10},{10,1... | collective-permute-start | bytes 122888 | tf_op jit(solution)/shard_map/ppermute | solution.py:233
  38.2 6.8 %collective-permute-start.12 = (bf16[160,128]{1,0:T(8,128)(2,1)S(1)}, bf16[160,128]{1,0:T(8,128)(2,1)S(1)}, u32[]{:S(2)}, u32[]{:S(2)}) collective-permute-start(bf16[160,128]{1,0:T(8,128)(2,1)S(1)} %get-tuple-element.17), channel_id=1, source_target_pairs={{0,2},{1,3},{2,0},{3,1},{4,6},{5,7},{6,4},{7,5},{8,10},{9,11},{10,... | collective-permute-start | bytes 122888 | tf_op jit(solution)/shard_map/ppermute | solution.py:233
  42.4 4.4 %collective-permute-start.13 = (bf16[160,128]{1,0:T(8,128)(2,1)S(1)}, bf16[160,128]{1,0:T(8,128)(2,1)S(1)}, u32[]{:S(2)}, u32[]{:S(2)}) collective-permute-start(bf16[160,128]{1,0:T(8,128)(2,1)S(1)} %get-tuple-element.18), channel_id=1, source_target_pairs={{0,3},{1,0},{2,1},{3,2},{4,7},{5,4},{6,5},{7,6},{8,11},{9,8},{10,9... | collective-permute-start | bytes 122888 | tf_op jit(solution)/shard_map/ppermute | solution.py:233
where the time goes:
time: 48.2 us; the launch traced here: 47.6 us
  starting transfers between devices  31.8 us (66%)
  Pallas kernels  8.86 us (18%)
  waiting for transfers between devices  2.9 us (6%)
  local copies, waits for them, and re-layouts  2.65 us (5%)
  between operations  0.78 us (2%)
    ppermute x4, starting transfers between devices, gather_window(): lax.ppermute(piece, 'tmpl', pairs_of(lambda z, y, x, c: (z, y, x, c + 1)))  10.6 us
    ppermute x3, starting transfers between devices, on_device(): lax.ppermute(parts[d], 'sta', [(i, (i + d) % 4) for i in range(4)])  9.69 us
    ppermute x6, starting transfers between devices, spread(): came.append(lax.ppermute(block, 'tmpl', pairs_of(move)))  9.05 us
    pallas_call x1, Pallas kernels, correlate(): pl.pallas_call(correlate_kernel, out_shape=[jax.ShapeDtypeStruct((HELD *...  5.4 us
    pallas_call x1, Pallas kernels, toeplitz(): pl.pallas_call(toeplitz_kernel, out_shape=jax.ShapeDtypeStruct((CHANS, 51...  2.74 us
    ppermute x1, starting transfers between devices, gather_window(): lax.ppermute(window, 'tmpl', pairs_of(lambda z, y, x, c: (z + 1, y, x, c)))  2.46 us
    ppermute x3, waiting for transfers between devices, on_device(): lax.ppermute(parts[d], 'sta', [(i, (i + d) % 4) for i in range(4)])  2.04 us
    dynamic_slice x1, local copies, waits for them, and re-layouts, normalized_templates(): lax.dynamic_index_in_dim(library, library_index[0], 0, keepdims=False)  1.15 us
  transfers between devices with their start and end apart: 14, of which 3 were waited for; matrix products, arithmetic and copies ran while one was open for 7% of the time, Pallas kernels for 6%

commit v1 on v0

--- a/solution.py
+++ b/solution.py
@@ -78,7 +78,7 @@
                 both = jnp.concatenate(halves, axis=0).astype(jnp.bfloat16)
                 for q in range(4):
                     b = -q % 4
-                    out_ref[c, 128 * q + 16 * pair : 128 * q + 16 * pair + 16, :] = both[:, 128 * b : 128 * b + 128]
+                    out_ref[c, 16 * pair : 16 * pair + 16, 128 * q : 128 * q + 128] = both[:, 128 * b : 128 * b + 128]
         return carry
 
     lax.fori_loop(0, CHANS // BUNCH, several, 0)
@@ -90,7 +90,7 @@
     turned = jnp.dot(taps, (((row + column) & 511) == 0).astype(jnp.bfloat16), preferred_element_type=jnp.float32)
     return pl.pallas_call(
         toeplitz_kernel,
-        out_shape=jax.ShapeDtypeStruct((CHANS, 512, 128), jnp.bfloat16),
+        out_shape=jax.ShapeDtypeStruct((CHANS, 128, 512), jnp.bfloat16),
         in_specs=[pl.BlockSpec(memory_space=pltpu.VMEM), pl.BlockSpec(memory_space=pl.ANY)],
         out_specs=pl.BlockSpec(memory_space=pltpu.VMEM),
         compiler_params=pltpu.CompilerParams(vmem_limit_bytes=16 << 20),
@@ -100,14 +100,13 @@
 
 def correlate_kernel(
     meta_ref, m0_ref, m1_ref, m2_ref, m3_ref, n0_ref, n1_ref, n2_ref, n3_ref, toep_ref,
-    o0_ref, o1_ref, o2_ref, o3_ref, rows_ref, inverse_ref, square_ref, shift_ref, acc_ref, band_ref,
+    o0_ref, o1_ref, o2_ref, o3_ref, rows_ref, inverse_ref, square_ref, shift_ref, acc_ref, band_ref, later_ref,
 ):
     z0, y0, x0, c0, s0 = (meta_ref[k] for k in range(5))
     acc_ref[...] = jnp.zeros_like(acc_ref)
     band_ref[...] = window_band()
+    later_ref[:, 64:, :] = jnp.zeros((3 * BUNCH, PITCH - 64, 128), jnp.float32)
     square_ref[64 * ROWS : 65 * ROWS, :] = jnp.zeros((ROWS, 128), jnp.bfloat16)
-    for r in (64, 65, 66):
-        rows_ref[pl.ds(r, CHANS, stride=PITCH), :] = jnp.zeros((CHANS, 128), jnp.float32)
     pieces = ((m0_ref, n0_ref), (m1_ref, n1_ref), (m2_ref, n2_ref), (m3_ref, n3_ref))
     for dy, both in enumerate(pieces):
         for dx in range(4):
@@ -140,19 +139,24 @@
         for k in range(BUNCH):
             c = step * BUNCH + k
             base = pl.multiple_of(c * PITCH, 8)
-            values = jnp.concatenate(
-                [rows_ref[pl.ds(base + q, 64), :].astype(jnp.bfloat16) for q in range(4)], axis=1
+            parts = lax.dot_general(
+                rows_ref[pl.ds(base, 64), :].astype(jnp.bfloat16),
+                toep_ref[c],
+                (((1,), (0,)), ((), ())),
+                preferred_element_type=jnp.float32,
             )
-            corr = lax.dot_general(
-                values, toep_ref[c], (((1,), (0,)), ((), ())), preferred_element_type=jnp.float32
-            )
-            shift_ref[k, :64, :] = corr * inverse_ref[pl.ds(base, 64), :]
+            corr = parts[:, :128]
+            for q in (1, 2, 3):
+                later_ref[3 * k + q - 1, :64, :] = parts[:, 128 * q : 128 * q + 128]
+            for q in (1, 2, 3):
+                corr = corr + later_ref[3 * k + q - 1, q : q + 64, :]
             move = meta_ref[5 + c]
             skip, turn = move >> 7, move & 127
             back = (128 - turn) & 127
-            low = pltpu.roll(shift_ref[k, pl.ds(skip, 64), :], back, axis=1)
-            high = pltpu.roll(shift_ref[k, pl.ds(skip + 1, 64), :], back, axis=1)
-            moved = jnp.where(lane < 128 - turn, low, high)
+            shift_ref[k, :64, :] = pltpu.roll(corr * inverse_ref[pl.ds(base, 64), :], back, axis=1)
+            moved = jnp.where(
+                lane < 128 - turn, shift_ref[k, pl.ds(skip, 64), :], shift_ref[k, pl.ds(skip + 1, 64), :]
+            )
             moved = jnp.where(line < 60, moved, 1.0)
             start = pl.multiple_of((meta_ref[5 + CHANS + c] - 2 * s0) * 64, 64)
             acc_ref[pl.ds(start, 64), :] += moved
@@ -208,6 +212,7 @@
             pltpu.VMEM((BUNCH, PITCH, 128), jnp.float32),
             pltpu.VMEM((HELD * 64, 128), jnp.float32),
             pltpu.VMEM((256, 256), jnp.bfloat16),
+            pltpu.VMEM((3 * BUNCH, PITCH, 128), jnp.float32),
         ],
         compiler_params=pltpu.CompilerParams(vmem_limit_bytes=32 << 20),
     )(meta, *pieces, toep)

time: 48.2 us -> 47.7 us (0.990)
  no operation moved by 1% of the time
where the time goes in v1:
time: 47.7 us; the launch traced here: 47.1 us
  starting transfers between devices  31.7 us (66%)
  Pallas kernels  8.4 us (18%)
  waiting for transfers between devices  2.92 us (6%)
  local copies, waits for them, and re-layouts  2.65 us (6%)
  between operations  0.78 us (2%)
    ppermute x4, starting transfers between devices, gather_window(): lax.ppermute(piece, 'tmpl', pairs_of(lambda z, y, x, c: (z, y, x, c + 1)))  10.6 us
    ppermute x3, starting transfers between devices, on_device(): lax.ppermute(parts[d], 'sta', [(i, (i + d) % 4) for i in range(4)])  9.66 us
    ppermute x6, starting transfers between devices, spread(): came.append(lax.ppermute(block, 'tmpl', pairs_of(move)))  9.05 us
    pallas_call x1, Pallas kernels, correlate(): pl.pallas_call(correlate_kernel, out_shape=[jax.ShapeDtypeStruct((HELD *...  4.93 us
    pallas_call x1, Pallas kernels, toeplitz(): pl.pallas_call(toeplitz_kernel, out_shape=jax.ShapeDtypeStruct((CHANS, 12...  2.75 us
    ppermute x1, starting transfers between devices, gather_window(): lax.ppermute(window, 'tmpl', pairs_of(lambda z, y, x, c: (z + 1, y, x, c)))  2.46 us
    ppermute x3, waiting for transfers between devices, on_device(): lax.ppermute(parts[d], 'sta', [(i, (i + d) % 4) for i in range(4)])  2.05 us
    dynamic_slice x1, local copies, waits for them, and re-layouts, normalized_templates(): lax.dynamic_index_in_dim(library, library_index[0], 0, keepdims=False)  1.15 us
  transfers between devices with their start and end apart: 14, of which 3 were waited for; matrix products, arithmetic and copies ran while one was open for 7% of the time, Pallas kernels for 6%

profile of v1, /device:TPU:1, one launch (start us, length us, event | category | flops | bytes accessed | tf_op | source)
XLA Modules:
  0.0 47.1 jit_solution(7800347181767286106)
XLA Ops:
  0.0 2.5 %collective-permute-start = (bf16[75,128]{1,0:T(8,128)(2,1)}, bf16[75,128]{1,0:T(8,128)(2,1)S(1)}, u32[]{:S(2)}, u32[]{:S(2)}) collective-permute-start(bf16[75,128]{1,0:T(8,128)(2,1)} %param.5), channel_id=1, source_target_pairs={{0,128},{4,132},{8,136},{12,140},{16,144},{20,148},{24,152},{28,15... | collective-permute-start | bytes 57608 | tf_op jit(solution)/shard_map/ppermute | solution.py:56
  3.1 1.1 %constant_dynamic-slice_fusion = bf16[1,75,300]{2,0,1:T(2,128)(2,1)S(1)} fusion(bf16[64,75,300]{2,0,1:T(8,128)(2,1)} %param.6, s32[]{:T(128)S(6)} %select_n.4), kind=kLoop, calls=%fused_computation.18 | loop fusion | bytes 90004 | tf_op jit(solution)/shard_map/jit(dynamic_index_in_dim)/dynamic_slice | solution.py:22
  4.3 0.1 convert_reduce_fusion
  4.4 0.2 fusion.6
  4.6 0.7 %pad_bitcast_fusion.1 = bf16[1,80,128]{2,1,0:T(8,128)(2,1)S(1)} fusion(bf16[75,128]{1,0:T(8,128)(2,1)} %param.5), kind=kLoop, calls=%fused_computation.14 | loop fusion | bytes 39680 | tf_op jit(solution)/shard_map/broadcast_in_dim | solution.py:52
  5.3 0.0 collective-permute-done
  5.4 2.8 %collective-permute-start.2 = (bf16[2,80,128]{2,1,0:T(8,128)(2,1)S(1)}, bf16[2,80,128]{2,1,0:T(8,128)(2,1)S(1)}, u32[]{:S(2)}, u32[]{:S(2)}) collective-permute-start(bf16[2,80,128]{2,1,0:T(8,128)(2,1)S(1)} %get-tuple-element.20), channel_id=1, source_target_pairs={{0,16},{4,20},{8,24},{12,28},{16,0},{20,4},{24,8},{28,12},{32,48},... | collective-permute-start | bytes 122888 | tf_op jit(solution)/shard_map/ppermute | solution.py:47
  8.2 0.3 collective-permute-start.1
  8.5 2.4 %collective-permute-start.3 = (bf16[2,80,128]{2,1,0:T(8,128)(2,1)S(1)}, bf16[2,80,128]{2,1,0:T(8,128)(2,1)S(1)}, u32[]{:S(2)}, u32[]{:S(2)}) collective-permute-start(bf16[2,80,128]{2,1,0:T(8,128)(2,1)S(1)} %get-tuple-element.20), channel_id=1, source_target_pairs={{0,24},{4,28},{8,0},{12,4},{16,8},{20,12},{24,16},{28,20},{32,56},... | collective-permute-start | bytes 122888 | tf_op jit(solution)/shard_map/ppermute | solution.py:47
  10.9 0.1 fusion.7
  11.0 0.8 %concatenate.11.meta_ref = s32[155]{0:T(256)S(1)} concatenate(s32[1]{0:T(128)} %bitcast.9, s32[1]{0:T(128)} %bitcast.10, s32[1]{0:T(128)} %bitcast.11, s32[1]{0:T(128)} %bitcast.12, s32[1]{0:T(128)} %bitcast.13, s32[75]{0:T(128)} %bitcast.42, s32[75]{0:T(128)} %param.9), dimensions={0} | concatenate | bytes 1240 | tf_op jit(solution)/shard_map/concatenate | solution.py:233
  11.7 0.0 collective-permute-done.2
  11.7 0.8 %collective-permute-done.1 = bf16[2,80,128]{2,1,0:T(8,128)(2,1)S(1)} collective-permute-done((bf16[2,80,128]{2,1,0:T(8,128)(2,1)S(1)}, bf16[2,80,128]{2,1,0:T(8,128)(2,1)S(1)}, u32[]{:S(2)}, u32[]{:S(2)}) %collective-permute-start.1) | collective-permute-done | bytes 40992 | tf_op jit(solution)/shard_map/ppermute | solution.py:47
  12.6 0.0 collective-permute-done.3
  12.6 2.5 %collective-permute-start.6 = (bf16[8,80,128]{2,1,0:T(8,128)(2,1)S(1)}, bf16[8,80,128]{2,1,0:T(8,128)(2,1)S(1)}, u32[]{:S(2)}, u32[]{:S(2)}) collective-permute-start(bf16[8,80,128]{2,1,0:T(8,128)(2,1)S(1)} %bitcast.34), channel_id=1, source_target_pairs={{0,96},{4,100},{8,104},{12,108},{16,112},{20,116},{24,120},{28,124... | collective-permute-start | bytes 491528 | tf_op jit(solution)/shard_map/ppermute | solution.py:47
  15.1 0.3 collective-permute-start.5
  15.4 0.7 %collective-permute-start.4 = (bf16[8,80,128]{2,1,0:T(8,128)(2,1)S(1)}, bf16[8,80,128]{2,1,0:T(8,128)(2,1)S(1)}, u32[]{:S(2)}, u32[]{:S(2)}) collective-permute-start(bf16[8,80,128]{2,1,0:T(8,128)(2,1)S(1)} %bitcast.36), channel_id=1, source_target_pairs={{0,32},{4,36},{8,40},{12,44},{16,48},{20,52},{24,56},{28,60},{32,6... | collective-permute-start | bytes 491528 | tf_op jit(solution)/shard_map/ppermute | solution.py:47
  16.1 3.2 %collective-permute-start.7 = (bf16[8,80,128]{2,1,0:T(8,128)(2,1)S(1)}, bf16[8,80,128]{2,1,0:T(8,128)(2,1)S(1)}, u32[]{:S(2)}, u32[]{:S(2)}) collective-permute-start(bf16[8,80,128]{2,1,0:T(8,128)(2,1)S(1)} %bitcast.37), channel_id=1, source_target_pairs={{0,4},{4,0},{8,12},{12,8},{16,20},{20,16},{24,28},{28,24},{32,36},... | collective-permute-start | bytes 491528 | tf_op jit(solution)/shard_map/ppermute | solution.py:65
  19.4 0.0 collective-permute-done.6.m3_ref
  19.4 3.7 %collective-permute-start.10 = (bf16[8,80,128]{2,1,0:T(8,128)(2,1)S(1)}, bf16[8,80,128]{2,1,0:T(8,128)(2,1)S(1)}, u32[]{:S(2)}, u32[]{:S(2)}) collective-permute-start(bf16[8,80,128]{2,1,0:T(8,128)(2,1)S(1)} %collective-permute-done.6.m3_ref), channel_id=1, source_target_pairs={{0,4},{4,0},{8,12},{12,8},{16,20},{20,16},{24,28},{28,24},{32,36},... | collective-permute-start | bytes 491528 | tf_op jit(solution)/shard_map/ppermute | solution.py:65
  23.0 0.0 collective-permute-done.5.m2_ref
  23.1 2.0 %collective-permute-start.9 = (bf16[8,80,128]{2,1,0:T(8,128)(2,1)S(1)}, bf16[8,80,128]{2,1,0:T(8,128)(2,1)S(1)}, u32[]{:S(2)}, u32[]{:S(2)}) collective-permute-start(bf16[8,80,128]{2,1,0:T(8,128)(2,1)S(1)} %collective-permute-done.5.m2_ref), channel_id=1, source_target_pairs={{0,4},{4,0},{8,12},{12,8},{16,20},{20,16},{24,28},{28,24},{32,36},... | collective-permute-start | bytes 491528 | tf_op jit(solution)/shard_map/ppermute | solution.py:65
  25.1 0.0 collective-permute-done.4.m1_ref
  25.1 1.6 %collective-permute-start.8 = (bf16[8,80,128]{2,1,0:T(8,128)(2,1)S(1)}, bf16[8,80,128]{2,1,0:T(8,128)(2,1)S(1)}, u32[]{:S(2)}, u32[]{:S(2)}) collective-permute-start(bf16[8,80,128]{2,1,0:T(8,128)(2,1)S(1)} %collective-permute-done.4.m1_ref), channel_id=1, source_target_pairs={{0,4},{4,0},{8,12},{12,8},{16,20},{20,16},{24,28},{28,24},{32,36},... | collective-permute-start | bytes 491528 | tf_op jit(solution)/shard_map/ppermute | solution.py:65
  26.7 0.2 fusion.taps_ref
  26.9 2.7 %shard_map.55.toep_ref = bf16[75,128,512]{2,1,0:T(8,128)(2,1)S(1)} custom-call(f32[75,512]{1,0:T(8,128)S(1)} %fusion.taps_ref, s32[155]{0:T(256)S(1)} %concatenate.11.meta_ref), custom_call_target="tpu_custom_call" | custom-call | flops 39321600 | bytes 9830400 | tf_op jit(solution)/shard_map/pallas_call | solution.py:91
  29.7 0.0 collective-permute-done.7.n0_ref
  29.7 0.0 collective-permute-done.10.n3_ref
  29.7 0.0 collective-permute-done.9.n2_ref
  29.7 0.0 collective-permute-done.8.n1_ref
  29.7 4.9 %shard_map.56 = (bf16[160,128]{1,0:T(8,128)(2,1)S(1)}, bf16[160,128]{1,0:T(8,128)(2,1)S(1)}, bf16[160,128]{1,0:T(8,128)(2,1)S(1)}, bf16[160,128]{1,0:T(8,128)(2,1)S(1)}) custom-call(s32[155]{0:T(256)S(1)} %concatenate.11.meta_ref, bf16[8,80,128]{2,1,0:T(8,128)(2,1)S(1)} %bitcast.38, bf16[8,80,128]{2,1,0:T(8,128)(2,1)S(1)} %collective-permute-done.4.m1_ref, ...), custom_call_target="tpu_custom_call" | custom-call | tf_op jit(solution)/shard_map/pallas_call | solution.py:203
  34.6 3.1 %collective-permute-start.11 = (bf16[160,128]{1,0:T(8,128)(2,1)S(1)}, bf16[160,128]{1,0:T(8,128)(2,1)S(1)}, u32[]{:S(2)}, u32[]{:S(2)}) collective-permute-start(bf16[160,128]{1,0:T(8,128)(2,1)S(1)} %get-tuple-element.16), channel_id=1, source_target_pairs={{0,1},{1,2},{2,3},{3,0},{4,5},{5,6},{6,7},{7,4},{8,9},{9,10},{10,1... | collective-permute-start | bytes 122888 | tf_op jit(solution)/shard_map/ppermute | solution.py:238
  37.7 4.2 %collective-permute-start.12 = (bf16[160,128]{1,0:T(8,128)(2,1)S(1)}, bf16[160,128]{1,0:T(8,128)(2,1)S(1)}, u32[]{:S(2)}, u32[]{:S(2)}) collective-permute-start(bf16[160,128]{1,0:T(8,128)(2,1)S(1)} %get-tuple-element.17), channel_id=1, source_target_pairs={{0,2},{1,3},{2,0},{3,1},{4,6},{5,7},{6,4},{7,5},{8,10},{9,11},{10,... | collective-permute-start | bytes 122888 | tf_op jit(solution)/shard_map/ppermute | solution.py:238
  41.9 2.4 %collective-permute-start.13 = (bf16[160,128]{1,0:T(8,128)(2,1)S(1)}, bf16[160,128]{1,0:T(8,128)(2,1)S(1)}, u32[]{:S(2)}, u32[]{:S(2)}) collective-permute-start(bf16[160,128]{1,0:T(8,128)(2,1)S(1)} %get-tuple-element.18), channel_id=1, source_target_pairs={{0,3},{1,0},{2,1},{3,2},{4,7},{5,4},{6,5},{7,6},{8,11},{9,8},{10,9... | collective-permute-start | bytes 122888 | tf_op jit(solution)/shard_map/ppermute | solution.py:238
  44.3 0.0 collective-permute-done.11.p1_ref
  44.3 0.2 collective-permute-done.12.p2_ref
  44.5 1.9 %collective-permute-done.13.p3_ref = bf16[160,128]{1,0:T(8,128)(2,1)S(1)} collective-permute-done((bf16[160,128]{1,0:T(8,128)(2,1)S(1)}, bf16[160,128]{1,0:T(8,128)(2,1)S(1)}, u32[]{:S(2)}, u32[]{:S(2)}) %collective-permute-start.13) | collective-permute-done | bytes 40992 | tf_op jit(solution)/shard_map/ppermute | solution.py:238
  46.4 0.7 %shard_map.57 = bf16[16,1920]{1,0:T(8,128)(2,1)} custom-call(bf16[160,128]{1,0:T(8,128)(2,1)S(1)} %get-tuple-element.15.p0_ref, bf16[160,128]{1,0:T(8,128)(2,1)S(1)} %collective-permute-done.11.p1_ref, bf16[160,128]{1,0:T(8,128)(2,1)S(1)} %collective-permute-done.12.p2_ref, bf16[160,128]{1,0:T(8,128)(2,1)S(1)} %collective-permute-done.13.p3_ref), custom_call_target="tpu_custom_call" | custom-call | tf_op jit(solution)/shard_map/pallas_call | solution.py:190
  (5 shorter events, 0.0 us)
Async XLA Ops:
  0.0 5.3 %collective-permute-start = (bf16[75,128]{1,0:T(8,128)(2,1)}, bf16[75,128]{1,0:T(8,128)(2,1)S(1)}, u32[]{:S(2)}, u32[]{:S(2)}) collective-permute-start(bf16[75,128]{1,0:T(8,128)(2,1)} %param.5), channel_id=1, source_target_pairs={{0,128},{4,132},{8,136},{12,140},{16,144},{20,148},{24,152},{28,15... | collective-permute-start | bytes 57608 | tf_op jit(solution)/shard_map/ppermute | solution.py:56
  5.4 6.4 %collective-permute-start.2 = (bf16[2,80,128]{2,1,0:T(8,128)(2,1)S(1)}, bf16[2,80,128]{2,1,0:T(8,128)(2,1)S(1)}, u32[]{:S(2)}, u32[]{:S(2)}) collective-permute-start(bf16[2,80,128]{2,1,0:T(8,128)(2,1)S(1)} %get-tuple-element.20), channel_id=1, source_target_pairs={{0,16},{4,20},{8,24},{12,28},{16,0},{20,4},{24,8},{28,12},{32,48},... | collective-permute-start | bytes 122888 | tf_op jit(solution)/shard_map/ppermute | solution.py:47
  8.2 4.4 %collective-permute-start.1 = (bf16[2,80,128]{2,1,0:T(8,128)(2,1)S(1)}, bf16[2,80,128]{2,1,0:T(8,128)(2,1)S(1)}, u32[]{:S(2)}, u32[]{:S(2)}) collective-permute-start(bf16[2,80,128]{2,1,0:T(8,128)(2,1)S(1)} %get-tuple-element.20), channel_id=1, source_target_pairs={{0,8},{4,12},{8,16},{12,20},{16,24},{20,28},{24,0},{28,4},{32,40},... | collective-permute-start | bytes 122888 | tf_op jit(solution)/shard_map/ppermute | solution.py:47
  8.5 4.1 %collective-permute-start.3 = (bf16[2,80,128]{2,1,0:T(8,128)(2,1)S(1)}, bf16[2,80,128]{2,1,0:T(8,128)(2,1)S(1)}, u32[]{:S(2)}, u32[]{:S(2)}) collective-permute-start(bf16[2,80,128]{2,1,0:T(8,128)(2,1)S(1)} %get-tuple-element.20), channel_id=1, source_target_pairs={{0,24},{4,28},{8,0},{12,4},{16,8},{20,12},{24,16},{28,20},{32,56},... | collective-permute-start | bytes 122888 | tf_op jit(solution)/shard_map/ppermute | solution.py:47
  12.6 6.8 %collective-permute-start.6 = (bf16[8,80,128]{2,1,0:T(8,128)(2,1)S(1)}, bf16[8,80,128]{2,1,0:T(8,128)(2,1)S(1)}, u32[]{:S(2)}, u32[]{:S(2)}) collective-permute-start(bf16[8,80,128]{2,1,0:T(8,128)(2,1)S(1)} %bitcast.34), channel_id=1, source_target_pairs={{0,96},{4,100},{8,104},{12,108},{16,112},{20,116},{24,120},{28,124... | collective-permute-start | bytes 491528 | tf_op jit(solution)/shard_map/ppermute | solution.py:47
  15.1 8.0 %collective-permute-start.5 = (bf16[8,80,128]{2,1,0:T(8,128)(2,1)S(1)}, bf16[8,80,128]{2,1,0:T(8,128)(2,1)S(1)}, u32[]{:S(2)}, u32[]{:S(2)}) collective-permute-start(bf16[8,80,128]{2,1,0:T(8,128)(2,1)S(1)} %bitcast.35), channel_id=1, source_target_pairs={{0,64},{4,68},{8,72},{12,76},{16,80},{20,84},{24,88},{28,92},{32,9... | collective-permute-start | bytes 491528 | tf_op jit(solution)/shard_map/ppermute | solution.py:47
  15.4 9.6 %collective-permute-start.4 = (bf16[8,80,128]{2,1,0:T(8,128)(2,1)S(1)}, bf16[8,80,128]{2,1,0:T(8,128)(2,1)S(1)}, u32[]{:S(2)}, u32[]{:S(2)}) collective-permute-start(bf16[8,80,128]{2,1,0:T(8,128)(2,1)S(1)} %bitcast.36), channel_id=1, source_target_pairs={{0,32},{4,36},{8,40},{12,44},{16,48},{20,52},{24,56},{28,60},{32,6... | collective-permute-start | bytes 491528 | tf_op jit(solution)/shard_map/ppermute | solution.py:47
  16.1 13.5 %collective-permute-start.7 = (bf16[8,80,128]{2,1,0:T(8,128)(2,1)S(1)}, bf16[8,80,128]{2,1,0:T(8,128)(2,1)S(1)}, u32[]{:S(2)}, u32[]{:S(2)}) collective-permute-start(bf16[8,80,128]{2,1,0:T(8,128)(2,1)S(1)} %bitcast.37), channel_id=1, source_target_pairs={{0,4},{4,0},{8,12},{12,8},{16,20},{20,16},{24,28},{28,24},{32,36},... | collective-permute-start | bytes 491528 | tf_op jit(solution)/shard_map/ppermute | solution.py:65
  19.4 10.3 %collective-permute-start.10 = (bf16[8,80,128]{2,1,0:T(8,128)(2,1)S(1)}, bf16[8,80,128]{2,1,0:T(8,128)(2,1)S(1)}, u32[]{:S(2)}, u32[]{:S(2)}) collective-permute-start(bf16[8,80,128]{2,1,0:T(8,128)(2,1)S(1)} %collective-permute-done.6.m3_ref), channel_id=1, source_target_pairs={{0,4},{4,0},{8,12},{12,8},{16,20},{20,16},{24,28},{28,24},{32,36},... | collective-permute-start | bytes 491528 | tf_op jit(solution)/shard_map/ppermute | solution.py:65
  23.1 6.6 %collective-permute-start.9 = (bf16[8,80,128]{2,1,0:T(8,128)(2,1)S(1)}, bf16[8,80,128]{2,1,0:T(8,128)(2,1)S(1)}, u32[]{:S(2)}, u32[]{:S(2)}) collective-permute-start(bf16[8,80,128]{2,1,0:T(8,128)(2,1)S(1)} %collective-permute-done.5.m2_ref), channel_id=1, source_target_pairs={{0,4},{4,0},{8,12},{12,8},{16,20},{20,16},{24,28},{28,24},{32,36},... | collective-permute-start | bytes 491528 | tf_op jit(solution)/shard_map/ppermute | solution.py:65
  25.1 4.6 %collective-permute-start.8 = (bf16[8,80,128]{2,1,0:T(8,128)(2,1)S(1)}, bf16[8,80,128]{2,1,0:T(8,128)(2,1)S(1)}, u32[]{:S(2)}, u32[]{:S(2)}) collective-permute-start(bf16[8,80,128]{2,1,0:T(8,128)(2,1)S(1)} %collective-permute-done.4.m1_ref), channel_id=1, source_target_pairs={{0,4},{4,0},{8,12},{12,8},{16,20},{20,16},{24,28},{28,24},{32,36},... | collective-permute-start | bytes 491528 | tf_op jit(solution)/shard_map/ppermute | solution.py:65
  34.6 9.7 %collective-permute-start.11 = (bf16[160,128]{1,0:T(8,128)(2,1)S(1)}, bf16[160,128]{1,0:T(8,128)(2,1)S(1)}, u32[]{:S(2)}, u32[]{:S(2)}) collective-permute-start(bf16[160,128]{1,0:T(8,128)(2,1)S(1)} %get-tuple-element.16), channel_id=1, source_target_pairs={{0,1},{1,2},{2,3},{3,0},{4,5},{5,6},{6,7},{7,4},{8,9},{9,10},{10,1... | collective-permute-start | bytes 122888 | tf_op jit(solution)/shard_map/ppermute | solution.py:238
  37.7 6.8 %collective-permute-start.12 = (bf16[160,128]{1,0:T(8,128)(2,1)S(1)}, bf16[160,128]{1,0:T(8,128)(2,1)S(1)}, u32[]{:S(2)}, u32[]{:S(2)}) collective-permute-start(bf16[160,128]{1,0:T(8,128)(2,1)S(1)} %get-tuple-element.17), channel_id=1, source_target_pairs={{0,2},{1,3},{2,0},{3,1},{4,6},{5,7},{6,4},{7,5},{8,10},{9,11},{10,... | collective-permute-start | bytes 122888 | tf_op jit(solution)/shard_map/ppermute | solution.py:238
  41.9 4.4 %collective-permute-start.13 = (bf16[160,128]{1,0:T(8,128)(2,1)S(1)}, bf16[160,128]{1,0:T(8,128)(2,1)S(1)}, u32[]{:S(2)}, u32[]{:S(2)}) collective-permute-start(bf16[160,128]{1,0:T(8,128)(2,1)S(1)} %get-tuple-element.18), channel_id=1, source_target_pairs={{0,3},{1,0},{2,1},{3,2},{4,7},{5,4},{6,5},{7,6},{8,11},{9,8},{10,9... | collective-permute-start | bytes 122888 | tf_op jit(solution)/shard_map/ppermute | solution.py:238

commit v2 on v1

--- a/solution.py
+++ b/solution.py
@@ -1,3 +1,5 @@
+import functools
+
 import jax
 import jax.numpy as jnp
 from jax import lax
@@ -58,19 +60,21 @@
     part = join([jnp.pad(window, fill), jnp.pad(came, fill)])
     part = join(spread(part, [lambda z, y, x, c, d=d: (z, y, x + d, c) for d in (1, 2, 3)]))
     part, taps, meta = lax.optimization_barrier((part.reshape(8, ROWS, 128), taps, meta))
-    toep = toeplitz(taps, meta)
+    turned = turned_taps(taps)
+    early = toeplitz(turned, meta, 0, CHANS - BUNCH)
+    late = toeplitz(turned, meta, CHANS - BUNCH, BUNCH)
     part = spread(part, [lambda z, y, x, c, d=d: (z, y + d, x, c) for d in (1, 2, 3)])
     other = []
     for piece in part:
         other.append(lax.ppermute(piece, "tmpl", pairs_of(lambda z, y, x, c: (z, y, x, c + 1))))
-    return part + other, toep, meta
-
-
-def toeplitz_kernel(taps_ref, meta_ref, out_ref):
+    return part + other, early, late, meta
+
+
+def toeplitz_kernel(origin, count, taps_ref, meta_ref, out_ref):
     def several(step, carry):
         for k in range(BUNCH):
             c = step * BUNCH + k
-            base = jnp.broadcast_to(taps_ref[pl.ds(c, 1), :], (8, 512))
+            base = jnp.broadcast_to(taps_ref[pl.ds(origin + c, 1), :], (8, 512))
             for pair in range(8):
                 halves = [
                     pltpu.roll(base, 16 * pair + 8 * h, axis=1, stride=1, stride_axis=0) for h in (0, 1)
@@ -81,25 +85,28 @@
                     out_ref[c, 16 * pair : 16 * pair + 16, 128 * q : 128 * q + 128] = both[:, 128 * b : 128 * b + 128]
         return carry
 
-    lax.fori_loop(0, CHANS // BUNCH, several, 0)
-
-
-def toeplitz(taps, meta):
+    lax.fori_loop(0, count // BUNCH, several, 0)
+
+
+def turned_taps(taps):
     row = lax.broadcasted_iota(jnp.int32, (TMPL_LEN, 512), 0)
     column = lax.broadcasted_iota(jnp.int32, (TMPL_LEN, 512), 1)
-    turned = jnp.dot(taps, (((row + column) & 511) == 0).astype(jnp.bfloat16), preferred_element_type=jnp.float32)
+    return jnp.dot(taps, (((row + column) & 511) == 0).astype(jnp.bfloat16), preferred_element_type=jnp.float32)
+
+
+def toeplitz(turned, meta, origin, count):
     return pl.pallas_call(
-        toeplitz_kernel,
-        out_shape=jax.ShapeDtypeStruct((CHANS, 128, 512), jnp.bfloat16),
+        functools.partial(toeplitz_kernel, origin, count),
+        out_shape=jax.ShapeDtypeStruct((count, 128, 512), jnp.bfloat16),
         in_specs=[pl.BlockSpec(memory_space=pltpu.VMEM), pl.BlockSpec(memory_space=pl.ANY)],
         out_specs=pl.BlockSpec(memory_space=pltpu.VMEM),
         compiler_params=pltpu.CompilerParams(vmem_limit_bytes=16 << 20),
-        cost_estimate=pl.CostEstimate(flops=CHANS * 65536 * 8, bytes_accessed=CHANS * 131072, transcendentals=0),
+        cost_estimate=pl.CostEstimate(flops=count * 65536 * 8, bytes_accessed=count * 131072, transcendentals=0),
     )(turned, meta)
 
 
 def correlate_kernel(
-    meta_ref, m0_ref, m1_ref, m2_ref, m3_ref, n0_ref, n1_ref, n2_ref, n3_ref, toep_ref,
+    meta_ref, m0_ref, m1_ref, m2_ref, m3_ref, n0_ref, n1_ref, n2_ref, n3_ref, early_ref, late_ref,
     o0_ref, o1_ref, o2_ref, o3_ref, rows_ref, inverse_ref, square_ref, shift_ref, acc_ref, band_ref, later_ref,
 ):
     z0, y0, x0, c0, s0 = (meta_ref[k] for k in range(5))
@@ -135,13 +142,13 @@
     lane = lax.broadcasted_iota(jnp.int32, (64, 128), 1)
     line = lax.broadcasted_iota(jnp.int32, (64, 128), 0)
 
-    def bunch(step, carry):
+    def bunch(toep_ref, origin, step, carry):
         for k in range(BUNCH):
             c = step * BUNCH + k
             base = pl.multiple_of(c * PITCH, 8)
             parts = lax.dot_general(
                 rows_ref[pl.ds(base, 64), :].astype(jnp.bfloat16),
-                toep_ref[c],
+                toep_ref[c - origin],
                 (((1,), (0,)), ((), ())),
                 preferred_element_type=jnp.float32,
             )
@@ -162,7 +169,9 @@
             acc_ref[pl.ds(start, 64), :] += moved
         return carry
 
-    lax.fori_loop(0, CHANS // BUNCH, bunch, 0)
+    steps = CHANS // BUNCH - 1
+    lax.fori_loop(0, steps, functools.partial(bunch, early_ref, 0), 0)
+    bunch(late_ref, steps * BUNCH, steps, 0)
     last = lax.broadcasted_iota(jnp.int32, (8, 128), 0) == 7
     for d, out in enumerate((o0_ref, o1_ref, o2_ref, o3_ref)):
         origin = ((s0 + d) & 3) * 15
@@ -197,13 +206,13 @@
     )(*parts)
 
 
-def correlate(meta, pieces, toep):
+def correlate(meta, pieces, early, late):
     smem = pl.BlockSpec(memory_space=pltpu.SMEM)
     vmem = pl.BlockSpec(memory_space=pltpu.VMEM)
     return pl.pallas_call(
         correlate_kernel,
         out_shape=[jax.ShapeDtypeStruct((HELD * 16, 128), jnp.bfloat16)] * 4,
-        in_specs=[smem] + [vmem] * 9,
+        in_specs=[smem] + [vmem] * 10,
         out_specs=[vmem] * 4,
         scratch_shapes=[
             pltpu.VMEM((CHANS * PITCH, 128), jnp.float32),
@@ -215,7 +224,7 @@
             pltpu.VMEM((3 * BUNCH, PITCH, 128), jnp.float32),
         ],
         compiler_params=pltpu.CompilerParams(vmem_limit_bytes=32 << 20),
-    )(meta, *pieces, toep)
+    )(meta, *pieces, early, late)
 
 
 def window_band():
@@ -231,8 +240,8 @@
     taps = normalized_templates(library, library_index)
     place = jnp.stack([me >> 5, (me >> 3) & 3, (me >> 1) & 3, me & 1, lax.axis_index("sta")]).astype(jnp.int32)
     meta = jnp.concatenate([place, moveout[0], group_of])
-    pieces, toep, meta = gather_window(window, taps, meta)
-    parts = correlate(meta, pieces, toep)
+    pieces, early, late, meta = gather_window(window, taps, meta)
+    parts = correlate(meta, pieces, early, late)
     came = [parts[0]]
     for d in (1, 2, 3):
         came.append(lax.ppermute(parts[d], "sta", [(i, (i + d) % 4) for i in range(4)]))

time: 47.7 us -> 47.7 us (level)
    pallas_call x1 -> x2, Pallas kernels: 2.75 us -> 2.74 us  [toeplitz(): pl.pallas_call(functools.partial(toeplitz_kernel, origin, count), out_sha...]
where the time goes in v2:
time: 47.7 us; the launch traced here: 47 us
  starting transfers between devices  31.7 us (66%)
  Pallas kernels  8.34 us (17%)
  waiting for transfers between devices  2.9 us (6%)
  local copies, waits for them, and re-layouts  2.65 us (6%)
  between operations  0.79 us (2%)
    ppermute x4, starting transfers between devices, gather_window(): lax.ppermute(piece, 'tmpl', pairs_of(lambda z, y, x, c: (z, y, x, c + 1)))  10.6 us
    ppermute x3, starting transfers between devices, on_device(): lax.ppermute(parts[d], 'sta', [(i, (i + d) % 4) for i in range(4)])  9.67 us
    ppermute x6, starting transfers between devices, spread(): came.append(lax.ppermute(block, 'tmpl', pairs_of(move)))  9.05 us
    pallas_call x1, Pallas kernels, correlate(): pl.pallas_call(correlate_kernel, out_shape=[jax.ShapeDtypeStruct((HELD *...  4.88 us
    pallas_call x2, Pallas kernels, toeplitz(): pl.pallas_call(functools.partial(toeplitz_kernel, origin, count), out_sha...  2.74 us
    ppermute x1, starting transfers between devices, gather_window(): lax.ppermute(window, 'tmpl', pairs_of(lambda z, y, x, c: (z + 1, y, x, c)))  2.46 us
    ppermute x3, waiting for transfers between devices, on_device(): lax.ppermute(parts[d], 'sta', [(i, (i + d) % 4) for i in range(4)])  2.04 us
    dynamic_slice x1, local copies, waits for them, and re-layouts, normalized_templates(): lax.dynamic_index_in_dim(library, library_index[0], 0, keepdims=False)  1.15 us
  transfers between devices with their start and end apart: 14, of which 3 were waited for; matrix products, arithmetic and copies ran while one was open for 7% of the time, Pallas kernels for 6%

profile of v2, /device:TPU:1, one launch (start us, length us, event | category | flops | bytes accessed | tf_op | source)
XLA Modules:
  0.0 47.0 jit_solution(1755905330978381577)
XLA Ops:
  0.0 2.5 %collective-permute-start = (bf16[75,128]{1,0:T(8,128)(2,1)}, bf16[75,128]{1,0:T(8,128)(2,1)S(1)}, u32[]{:S(2)}, u32[]{:S(2)}) collective-permute-start(bf16[75,128]{1,0:T(8,128)(2,1)} %param.5), channel_id=1, source_target_pairs={{0,128},{4,132},{8,136},{12,140},{16,144},{20,148},{24,152},{28,15... | collective-permute-start | bytes 57608 | tf_op jit(solution)/shard_map/ppermute | solution.py:58
  3.1 1.1 %constant_dynamic-slice_fusion = bf16[1,75,300]{2,0,1:T(2,128)(2,1)S(1)} fusion(bf16[64,75,300]{2,0,1:T(8,128)(2,1)} %param.6, s32[]{:T(128)S(6)} %select_n.4), kind=kLoop, calls=%fused_computation.18 | loop fusion | bytes 90004 | tf_op jit(solution)/shard_map/jit(dynamic_index_in_dim)/dynamic_slice | solution.py:24
  4.3 0.1 convert_reduce_fusion
  4.4 0.2 fusion.6
  4.6 0.7 %pad_bitcast_fusion.1 = bf16[1,80,128]{2,1,0:T(8,128)(2,1)S(1)} fusion(bf16[75,128]{1,0:T(8,128)(2,1)} %param.5), kind=kLoop, calls=%fused_computation.14 | loop fusion | bytes 39680 | tf_op jit(solution)/shard_map/broadcast_in_dim | solution.py:54
  5.3 0.0 collective-permute-done
  5.4 2.8 %collective-permute-start.2 = (bf16[2,80,128]{2,1,0:T(8,128)(2,1)S(1)}, bf16[2,80,128]{2,1,0:T(8,128)(2,1)S(1)}, u32[]{:S(2)}, u32[]{:S(2)}) collective-permute-start(bf16[2,80,128]{2,1,0:T(8,128)(2,1)S(1)} %get-tuple-element.20), channel_id=1, source_target_pairs={{0,16},{4,20},{8,24},{12,28},{16,0},{20,4},{24,8},{28,12},{32,48},... | collective-permute-start | bytes 122888 | tf_op jit(solution)/shard_map/ppermute | solution.py:49
  8.2 0.3 collective-permute-start.1
  8.5 2.4 %collective-permute-start.3 = (bf16[2,80,128]{2,1,0:T(8,128)(2,1)S(1)}, bf16[2,80,128]{2,1,0:T(8,128)(2,1)S(1)}, u32[]{:S(2)}, u32[]{:S(2)}) collective-permute-start(bf16[2,80,128]{2,1,0:T(8,128)(2,1)S(1)} %get-tuple-element.20), channel_id=1, source_target_pairs={{0,24},{4,28},{8,0},{12,4},{16,8},{20,12},{24,16},{28,20},{32,56},... | collective-permute-start | bytes 122888 | tf_op jit(solution)/shard_map/ppermute | solution.py:49
  10.9 0.1 fusion.7
  11.0 0.8 %concatenate.11.meta_ref = s32[155]{0:T(256)S(1)} concatenate(s32[1]{0:T(128)} %bitcast.9, s32[1]{0:T(128)} %bitcast.10, s32[1]{0:T(128)} %bitcast.11, s32[1]{0:T(128)} %bitcast.12, s32[1]{0:T(128)} %bitcast.13, s32[75]{0:T(128)} %bitcast.42, s32[75]{0:T(128)} %param.9), dimensions={0} | concatenate | bytes 1240 | tf_op jit(solution)/shard_map/concatenate | solution.py:242
  11.7 0.0 collective-permute-done.2
  11.7 0.8 %collective-permute-done.1 = bf16[2,80,128]{2,1,0:T(8,128)(2,1)S(1)} collective-permute-done((bf16[2,80,128]{2,1,0:T(8,128)(2,1)S(1)}, bf16[2,80,128]{2,1,0:T(8,128)(2,1)S(1)}, u32[]{:S(2)}, u32[]{:S(2)}) %collective-permute-start.1) | collective-permute-done | bytes 40992 | tf_op jit(solution)/shard_map/ppermute | solution.py:49
  12.6 0.0 collective-permute-done.3
  12.6 2.5 %collective-permute-start.6 = (bf16[8,80,128]{2,1,0:T(8,128)(2,1)S(1)}, bf16[8,80,128]{2,1,0:T(8,128)(2,1)S(1)}, u32[]{:S(2)}, u32[]{:S(2)}) collective-permute-start(bf16[8,80,128]{2,1,0:T(8,128)(2,1)S(1)} %bitcast.34), channel_id=1, source_target_pairs={{0,96},{4,100},{8,104},{12,108},{16,112},{20,116},{24,120},{28,124... | collective-permute-start | bytes 491528 | tf_op jit(solution)/shard_map/ppermute | solution.py:49
  15.1 0.3 collective-permute-start.5
  15.4 0.7 %collective-permute-start.4 = (bf16[8,80,128]{2,1,0:T(8,128)(2,1)S(1)}, bf16[8,80,128]{2,1,0:T(8,128)(2,1)S(1)}, u32[]{:S(2)}, u32[]{:S(2)}) collective-permute-start(bf16[8,80,128]{2,1,0:T(8,128)(2,1)S(1)} %bitcast.36), channel_id=1, source_target_pairs={{0,32},{4,36},{8,40},{12,44},{16,48},{20,52},{24,56},{28,60},{32,6... | collective-permute-start | bytes 491528 | tf_op jit(solution)/shard_map/ppermute | solution.py:49
  16.1 3.2 %collective-permute-start.7 = (bf16[8,80,128]{2,1,0:T(8,128)(2,1)S(1)}, bf16[8,80,128]{2,1,0:T(8,128)(2,1)S(1)}, u32[]{:S(2)}, u32[]{:S(2)}) collective-permute-start(bf16[8,80,128]{2,1,0:T(8,128)(2,1)S(1)} %bitcast.37), channel_id=1, source_target_pairs={{0,4},{4,0},{8,12},{12,8},{16,20},{20,16},{24,28},{28,24},{32,36},... | collective-permute-start | bytes 491528 | tf_op jit(solution)/shard_map/ppermute | solution.py:69
  19.4 0.0 collective-permute-done.6.m3_ref
  19.4 3.7 %collective-permute-start.10 = (bf16[8,80,128]{2,1,0:T(8,128)(2,1)S(1)}, bf16[8,80,128]{2,1,0:T(8,128)(2,1)S(1)}, u32[]{:S(2)}, u32[]{:S(2)}) collective-permute-start(bf16[8,80,128]{2,1,0:T(8,128)(2,1)S(1)} %collective-permute-done.6.m3_ref), channel_id=1, source_target_pairs={{0,4},{4,0},{8,12},{12,8},{16,20},{20,16},{24,28},{28,24},{32,36},... | collective-permute-start | bytes 491528 | tf_op jit(solution)/shard_map/ppermute | solution.py:69
  23.0 0.0 collective-permute-done.5.m2_ref
  23.1 2.0 %collective-permute-start.9 = (bf16[8,80,128]{2,1,0:T(8,128)(2,1)S(1)}, bf16[8,80,128]{2,1,0:T(8,128)(2,1)S(1)}, u32[]{:S(2)}, u32[]{:S(2)}) collective-permute-start(bf16[8,80,128]{2,1,0:T(8,128)(2,1)S(1)} %collective-permute-done.5.m2_ref), channel_id=1, source_target_pairs={{0,4},{4,0},{8,12},{12,8},{16,20},{20,16},{24,28},{28,24},{32,36},... | collective-permute-start | bytes 491528 | tf_op jit(solution)/shard_map/ppermute | solution.py:69
  25.1 0.0 collective-permute-done.4.m1_ref
  25.1 1.6 %collective-permute-start.8 = (bf16[8,80,128]{2,1,0:T(8,128)(2,1)S(1)}, bf16[8,80,128]{2,1,0:T(8,128)(2,1)S(1)}, u32[]{:S(2)}, u32[]{:S(2)}) collective-permute-start(bf16[8,80,128]{2,1,0:T(8,128)(2,1)S(1)} %collective-permute-done.4.m1_ref), channel_id=1, source_target_pairs={{0,4},{4,0},{8,12},{12,8},{16,20},{20,16},{24,28},{28,24},{32,36},... | collective-permute-start | bytes 491528 | tf_op jit(solution)/shard_map/ppermute | solution.py:69
  26.7 0.2 fusion.taps_ref
  26.9 0.9 %shard_map.56.late_ref = bf16[25,128,512]{2,1,0:T(8,128)(2,1)S(1)} custom-call(f32[75,512]{1,0:T(8,128)S(1)} %fusion.taps_ref, s32[155]{0:T(256)S(1)} %concatenate.11.meta_ref), custom_call_target="tpu_custom_call" | custom-call | flops 13107200 | bytes 3276800 | tf_op jit(solution)/shard_map/pallas_call | solution.py:98
  27.8 1.8 %shard_map.55.early_ref = bf16[50,128,512]{2,1,0:T(8,128)(2,1)S(1)} custom-call(f32[75,512]{1,0:T(8,128)S(1)} %fusion.taps_ref, s32[155]{0:T(256)S(1)} %concatenate.11.meta_ref), custom_call_target="tpu_custom_call" | custom-call | flops 26214400 | bytes 6553600 | tf_op jit(solution)/shard_map/pallas_call | solution.py:98
  29.7 0.0 collective-permute-done.7.n0_ref
  29.7 0.0 collective-permute-done.10.n3_ref
  29.7 0.0 collective-permute-done.9.n2_ref
  29.7 0.0 collective-permute-done.8.n1_ref
  29.7 4.9 %shard_map.57 = (bf16[160,128]{1,0:T(8,128)(2,1)S(1)}, bf16[160,128]{1,0:T(8,128)(2,1)S(1)}, bf16[160,128]{1,0:T(8,128)(2,1)S(1)}, bf16[160,128]{1,0:T(8,128)(2,1)S(1)}) custom-call(s32[155]{0:T(256)S(1)} %concatenate.11.meta_ref, bf16[8,80,128]{2,1,0:T(8,128)(2,1)S(1)} %bitcast.38, bf16[8,80,128]{2,1,0:T(8,128)(2,1)S(1)} %collective-permute-done.4.m1_ref, ...), custom_call_target="tpu_custom_call" | custom-call | tf_op jit(solution)/shard_map/pallas_call | solution.py:212
  34.6 3.1 %collective-permute-start.11 = (bf16[160,128]{1,0:T(8,128)(2,1)S(1)}, bf16[160,128]{1,0:T(8,128)(2,1)S(1)}, u32[]{:S(2)}, u32[]{:S(2)}) collective-permute-start(bf16[160,128]{1,0:T(8,128)(2,1)S(1)} %get-tuple-element.16), channel_id=1, source_target_pairs={{0,1},{1,2},{2,3},{3,0},{4,5},{5,6},{6,7},{7,4},{8,9},{9,10},{10,1... | collective-permute-start | bytes 122888 | tf_op jit(solution)/shard_map/ppermute | solution.py:247
  37.7 4.2 %collective-permute-start.12 = (bf16[160,128]{1,0:T(8,128)(2,1)S(1)}, bf16[160,128]{1,0:T(8,128)(2,1)S(1)}, u32[]{:S(2)}, u32[]{:S(2)}) collective-permute-start(bf16[160,128]{1,0:T(8,128)(2,1)S(1)} %get-tuple-element.17), channel_id=1, source_target_pairs={{0,2},{1,3},{2,0},{3,1},{4,6},{5,7},{6,4},{7,5},{8,10},{9,11},{10,... | collective-permute-start | bytes 122888 | tf_op jit(solution)/shard_map/ppermute | solution.py:247
  41.9 2.4 %collective-permute-start.13 = (bf16[160,128]{1,0:T(8,128)(2,1)S(1)}, bf16[160,128]{1,0:T(8,128)(2,1)S(1)}, u32[]{:S(2)}, u32[]{:S(2)}) collective-permute-start(bf16[160,128]{1,0:T(8,128)(2,1)S(1)} %get-tuple-element.18), channel_id=1, source_target_pairs={{0,3},{1,0},{2,1},{3,2},{4,7},{5,4},{6,5},{7,6},{8,11},{9,8},{10,9... | collective-permute-start | bytes 122888 | tf_op jit(solution)/shard_map/ppermute | solution.py:247
  44.3 0.0 collective-permute-done.11.p1_ref
  44.3 0.2 collective-permute-done.12.p2_ref
  44.4 1.9 %collective-permute-done.13.p3_ref = bf16[160,128]{1,0:T(8,128)(2,1)S(1)} collective-permute-done((bf16[160,128]{1,0:T(8,128)(2,1)S(1)}, bf16[160,128]{1,0:T(8,128)(2,1)S(1)}, u32[]{:S(2)}, u32[]{:S(2)}) %collective-permute-start.13) | collective-permute-done | bytes 40992 | tf_op jit(solution)/shard_map/ppermute | solution.py:247
  46.3 0.7 %shard_map.58 = bf16[16,1920]{1,0:T(8,128)(2,1)} custom-call(bf16[160,128]{1,0:T(8,128)(2,1)S(1)} %get-tuple-element.15.p0_ref, bf16[160,128]{1,0:T(8,128)(2,1)S(1)} %collective-permute-done.11.p1_ref, bf16[160,128]{1,0:T(8,128)(2,1)S(1)} %collective-permute-done.12.p2_ref, bf16[160,128]{1,0:T(8,128)(2,1)S(1)} %collective-permute-done.13.p3_ref), custom_call_target="tpu_custom_call" | custom-call | tf_op jit(solution)/shard_map/pallas_call | solution.py:199
  (5 shorter events, 0.0 us)
Async XLA Ops:
  0.0 5.3 %collective-permute-start = (bf16[75,128]{1,0:T(8,128)(2,1)}, bf16[75,128]{1,0:T(8,128)(2,1)S(1)}, u32[]{:S(2)}, u32[]{:S(2)}) collective-permute-start(bf16[75,128]{1,0:T(8,128)(2,1)} %param.5), channel_id=1, source_target_pairs={{0,128},{4,132},{8,136},{12,140},{16,144},{20,148},{24,152},{28,15... | collective-permute-start | bytes 57608 | tf_op jit(solution)/shard_map/ppermute | solution.py:58
  5.4 6.4 %collective-permute-start.2 = (bf16[2,80,128]{2,1,0:T(8,128)(2,1)S(1)}, bf16[2,80,128]{2,1,0:T(8,128)(2,1)S(1)}, u32[]{:S(2)}, u32[]{:S(2)}) collective-permute-start(bf16[2,80,128]{2,1,0:T(8,128)(2,1)S(1)} %get-tuple-element.20), channel_id=1, source_target_pairs={{0,16},{4,20},{8,24},{12,28},{16,0},{20,4},{24,8},{28,12},{32,48},... | collective-permute-start | bytes 122888 | tf_op jit(solution)/shard_map/ppermute | solution.py:49
  8.2 4.4 %collective-permute-start.1 = (bf16[2,80,128]{2,1,0:T(8,128)(2,1)S(1)}, bf16[2,80,128]{2,1,0:T(8,128)(2,1)S(1)}, u32[]{:S(2)}, u32[]{:S(2)}) collective-permute-start(bf16[2,80,128]{2,1,0:T(8,128)(2,1)S(1)} %get-tuple-element.20), channel_id=1, source_target_pairs={{0,8},{4,12},{8,16},{12,20},{16,24},{20,28},{24,0},{28,4},{32,40},... | collective-permute-start | bytes 122888 | tf_op jit(solution)/shard_map/ppermute | solution.py:49
  8.5 4.1 %collective-permute-start.3 = (bf16[2,80,128]{2,1,0:T(8,128)(2,1)S(1)}, bf16[2,80,128]{2,1,0:T(8,128)(2,1)S(1)}, u32[]{:S(2)}, u32[]{:S(2)}) collective-permute-start(bf16[2,80,128]{2,1,0:T(8,128)(2,1)S(1)} %get-tuple-element.20), channel_id=1, source_target_pairs={{0,24},{4,28},{8,0},{12,4},{16,8},{20,12},{24,16},{28,20},{32,56},... | collective-permute-start | bytes 122888 | tf_op jit(solution)/shard_map/ppermute | solution.py:49
  12.6 6.8 %collective-permute-start.6 = (bf16[8,80,128]{2,1,0:T(8,128)(2,1)S(1)}, bf16[8,80,128]{2,1,0:T(8,128)(2,1)S(1)}, u32[]{:S(2)}, u32[]{:S(2)}) collective-permute-start(bf16[8,80,128]{2,1,0:T(8,128)(2,1)S(1)} %bitcast.34), channel_id=1, source_target_pairs={{0,96},{4,100},{8,104},{12,108},{16,112},{20,116},{24,120},{28,124... | collective-permute-start | bytes 491528 | tf_op jit(solution)/shard_map/ppermute | solution.py:49
  15.1 8.0 %collective-permute-start.5 = (bf16[8,80,128]{2,1,0:T(8,128)(2,1)S(1)}, bf16[8,80,128]{2,1,0:T(8,128)(2,1)S(1)}, u32[]{:S(2)}, u32[]{:S(2)}) collective-permute-start(bf16[8,80,128]{2,1,0:T(8,128)(2,1)S(1)} %bitcast.35), channel_id=1, source_target_pairs={{0,64},{4,68},{8,72},{12,76},{16,80},{20,84},{24,88},{28,92},{32,9... | collective-permute-start | bytes 491528 | tf_op jit(solution)/shard_map/ppermute | solution.py:49
  15.4 9.6 %collective-permute-start.4 = (bf16[8,80,128]{2,1,0:T(8,128)(2,1)S(1)}, bf16[8,80,128]{2,1,0:T(8,128)(2,1)S(1)}, u32[]{:S(2)}, u32[]{:S(2)}) collective-permute-start(bf16[8,80,128]{2,1,0:T(8,128)(2,1)S(1)} %bitcast.36), channel_id=1, source_target_pairs={{0,32},{4,36},{8,40},{12,44},{16,48},{20,52},{24,56},{28,60},{32,6... | collective-permute-start | bytes 491528 | tf_op jit(solution)/shard_map/ppermute | solution.py:49
  16.1 13.5 %collective-permute-start.7 = (bf16[8,80,128]{2,1,0:T(8,128)(2,1)S(1)}, bf16[8,80,128]{2,1,0:T(8,128)(2,1)S(1)}, u32[]{:S(2)}, u32[]{:S(2)}) collective-permute-start(bf16[8,80,128]{2,1,0:T(8,128)(2,1)S(1)} %bitcast.37), channel_id=1, source_target_pairs={{0,4},{4,0},{8,12},{12,8},{16,20},{20,16},{24,28},{28,24},{32,36},... | collective-permute-start | bytes 491528 | tf_op jit(solution)/shard_map/ppermute | solution.py:69
  19.4 10.3 %collective-permute-start.10 = (bf16[8,80,128]{2,1,0:T(8,128)(2,1)S(1)}, bf16[8,80,128]{2,1,0:T(8,128)(2,1)S(1)}, u32[]{:S(2)}, u32[]{:S(2)}) collective-permute-start(bf16[8,80,128]{2,1,0:T(8,128)(2,1)S(1)} %collective-permute-done.6.m3_ref), channel_id=1, source_target_pairs={{0,4},{4,0},{8,12},{12,8},{16,20},{20,16},{24,28},{28,24},{32,36},... | collective-permute-start | bytes 491528 | tf_op jit(solution)/shard_map/ppermute | solution.py:69
  23.1 6.6 %collective-permute-start.9 = (bf16[8,80,128]{2,1,0:T(8,128)(2,1)S(1)}, bf16[8,80,128]{2,1,0:T(8,128)(2,1)S(1)}, u32[]{:S(2)}, u32[]{:S(2)}) collective-permute-start(bf16[8,80,128]{2,1,0:T(8,128)(2,1)S(1)} %collective-permute-done.5.m2_ref), channel_id=1, source_target_pairs={{0,4},{4,0},{8,12},{12,8},{16,20},{20,16},{24,28},{28,24},{32,36},... | collective-permute-start | bytes 491528 | tf_op jit(solution)/shard_map/ppermute | solution.py:69
  25.1 4.6 %collective-permute-start.8 = (bf16[8,80,128]{2,1,0:T(8,128)(2,1)S(1)}, bf16[8,80,128]{2,1,0:T(8,128)(2,1)S(1)}, u32[]{:S(2)}, u32[]{:S(2)}) collective-permute-start(bf16[8,80,128]{2,1,0:T(8,128)(2,1)S(1)} %collective-permute-done.4.m1_ref), channel_id=1, source_target_pairs={{0,4},{4,0},{8,12},{12,8},{16,20},{20,16},{24,28},{28,24},{32,36},... | collective-permute-start | bytes 491528 | tf_op jit(solution)/shard_map/ppermute | solution.py:69
  34.6 9.7 %collective-permute-start.11 = (bf16[160,128]{1,0:T(8,128)(2,1)S(1)}, bf16[160,128]{1,0:T(8,128)(2,1)S(1)}, u32[]{:S(2)}, u32[]{:S(2)}) collective-permute-start(bf16[160,128]{1,0:T(8,128)(2,1)S(1)} %get-tuple-element.16), channel_id=1, source_target_pairs={{0,1},{1,2},{2,3},{3,0},{4,5},{5,6},{6,7},{7,4},{8,9},{9,10},{10,1... | collective-permute-start | bytes 122888 | tf_op jit(solution)/shard_map/ppermute | solution.py:247
  37.7 6.8 %collective-permute-start.12 = (bf16[160,128]{1,0:T(8,128)(2,1)S(1)}, bf16[160,128]{1,0:T(8,128)(2,1)S(1)}, u32[]{:S(2)}, u32[]{:S(2)}) collective-permute-start(bf16[160,128]{1,0:T(8,128)(2,1)S(1)} %get-tuple-element.17), channel_id=1, source_target_pairs={{0,2},{1,3},{2,0},{3,1},{4,6},{5,7},{6,4},{7,5},{8,10},{9,11},{10,... | collective-permute-start | bytes 122888 | tf_op jit(solution)/shard_map/ppermute | solution.py:247
  41.9 4.4 %collective-permute-start.13 = (bf16[160,128]{1,0:T(8,128)(2,1)S(1)}, bf16[160,128]{1,0:T(8,128)(2,1)S(1)}, u32[]{:S(2)}, u32[]{:S(2)}) collective-permute-start(bf16[160,128]{1,0:T(8,128)(2,1)S(1)} %get-tuple-element.18), channel_id=1, source_target_pairs={{0,3},{1,0},{2,1},{3,2},{4,7},{5,4},{6,5},{7,6},{8,11},{9,8},{10,9... | collective-permute-start | bytes 122888 | tf_op jit(solution)/shard_map/ppermute | solution.py:247
